TPU v7x, 128 devices: a whole 4x4x4 slice. The times are simulated.
128 devices in a mesh: smp: 32 (over x, z, y_lo), col: 2 (over core), slab: 2 (over y_hi).
Axes of the slice: x: 4, y: 4 (y_hi: 2, y_lo: 2; y = y_hi * 2 + y_lo), z: 4, core: 2. Of those that a mesh axis runs over, the one named last changes fastest.
Arguments:
- jacobian: bfloat16 [1024, 32, 16384], P('smp', 'slab', 'col'), may hold values from -0.005722046 to 0.005722046
- local_energy: float32 [1024], P('smp'), may hold values from -6 to 6
Outputs:
- update: float32 [32, 16384], P('slab', ('col', 'smp'))
All inputs are finite; a program needn't handle non-finite values.
Results may differ from a plain program's by a relative error of at most 0.0085.
Values may be sent and summed in bfloat16 or wider, within the bound.
A program may use at most 192 MiB of HBM per device.

v0:
```python
import jax
import jax.numpy as jnp
from jax import lax
from jax.sharding import PartitionSpec as P

SLABS = 32
SLAB_COLS = 16384


def shards(jacobian, local_energy):
    energies = lax.all_gather(local_energy, "smp", axis=0, tiled=True)
    jacobian, energies = lax.optimization_barrier((jacobian, energies))
    samples = energies.shape[0]
    root_count = jnp.sqrt(jnp.float32(samples))
    eps = (energies - jnp.mean(energies)) / root_count
    columns = lax.all_to_all(jacobian, "smp", split_axis=2, concat_axis=0, tiled=True)
    slab_count = columns.shape[1]
    width = columns.shape[2]
    values = columns.astype(jnp.float32)
    mean_row = jnp.mean(values, axis=0, keepdims=True)
    centered = (
        ((values - mean_row) / root_count).astype(jnp.bfloat16).reshape(samples, slab_count * width)
    )
    partial_gram = jnp.dot(centered, centered.T, preferred_element_type=jnp.float32)
    gram = lax.psum(partial_gram, ("smp", "col", "slab"))
    shift = 0.01 * jnp.trace(gram) / samples
    factor = jnp.linalg.cholesky(gram + shift * jnp.eye(samples, dtype=jnp.float32))
    middle = lax.linalg.triangular_solve(factor, eps[:, None], left_side=True, lower=True)
    coeffs = lax.linalg.triangular_solve(
        factor, middle, left_side=True, lower=True, transpose_a=True
    )[:, 0]
    delta = jnp.dot(coeffs, centered.astype(jnp.float32), precision=lax.Precision.HIGHEST)
    squared = jnp.dot(
        coeffs,
        jnp.dot(gram, coeffs, precision=lax.Precision.HIGHEST),
        precision=lax.Precision.HIGHEST,
    )
    limit = 0.3 * jnp.sqrt(jnp.float32(SLABS * SLAB_COLS))
    scaled = -jnp.minimum(1.0, limit / jnp.sqrt(squared)) * delta
    return scaled.reshape(slab_count, width)


def solution(mesh):
    in_specs = (P("smp", "slab", "col"), P("smp"))
    out_specs = P("slab", ("col", "smp"))
    return jax.shard_map(shards, mesh=mesh, in_specs=in_specs, out_specs=out_specs, check_vma=False)
```

profile of v0, /device:TPU:1, one launch (start us, length us, event | category | flops | bytes accessed | tf_op | source)
XLA Modules:
  0.0 905.1 jit_solution(12480278940735346125)
XLA Ops:
  9.3 70.8 %all-reduce.1 = f32[1024]{0:T(1024)S(1)} all-reduce(f32[1024]{0:T(1024)S(1)} %dynamic-update-slice.47), channel_id=1, replica_groups=mesh['smp'=32,'col'=2,'slab'=2] {'smp'}, use_global_device_ids=true, to_apply=%add.1 | all-reduce | flops 1024 | bytes 8192 | tf_op jit(solution)/shard_map/optimization_barrier | solution.py:12
  80.1 45.6 %copy.65 = bf16[32,16,8192]{0,1,2:T(8,128)(2,1)} copy(bf16[32,16,8192]{2,1,0:T(8,128)(2,1)} %param.2) | data formatting | bytes 16777216 | tf_op jit(solution)/shard_map/optimization_barrier | solution.py:12
  125.7 39.8 %reshape.346 = bf16[32,2,65536]{2,1,0:T(2,128)(2,1)} reshape(bf16[8192,16,32]{2,1,0:T(8,128)(2,1)} %bitcast.343) | data formatting | bytes 16777216
  165.5 86.4 %all_to_all.4 = bf16[32,2,65536]{2,1,0:T(2,128)(2,1)} all-to-all(bf16[32,2,65536]{2,1,0:T(2,128)(2,1)} %reshape.346), channel_id=1, replica_groups=mesh['smp'=32,'col'=2,'slab'=2] {'smp'}, dimensions={0} | all-to-all | bytes 16777216 | tf_op jit(solution)/shard_map/all_to_all | solution.py:16
  251.9 30.6 %reshape.347 = bf16[8192,16,32]{2,1,0:T(8,128)(2,1)} reshape(bf16[32,2,65536]{2,1,0:T(2,128)(2,1)} %all_to_all.4) | data formatting | bytes 16777216
  282.5 44.0 %copy.66 = f32[32,16,32,256]{3,1,0,2:T(8,128)} copy(bf16[32,16,32,256]{0,1,3,2:T(8,128)(2,1)} %bitcast.342) | data formatting | bytes 25165824 | tf_op jit(solution)/shard_map/convert_element_type | solution.py:19
  343.8 16.8 %fusion.5 = f32[1024,1024]{0,1:T(8,128)} fusion(bf16[1024,16,256]{2,1,0:T(8,128)(2,1)S(1)} %bitcast.345), kind=kOutput, calls=%fused_computation.15 | convolution fusion | flops 8589934592 | bytes 12582912 | tf_op jit(solution)/shard_map/dot_general | solution.py:24
  362.1 12.2 %copy.98 = bf16[128,8,16,256]{3,1,2,0:T(8,128)(2,1)} copy(bf16[128,8,16,256]{3,2,1,0:T(8,128)(2,1)} %bitcast.346) | data formatting | bytes 16777216
  374.3 155.4 %all-reduce.4.cloned.1.call-done = f32[1024,1024]{0,1:T(8,128)} async-done(((f32[1024,1024]{0,1:T(8,128)}), f32[1024,1024]{0,1:T(8,128)}) %all-reduce.4.cloned.1.call-update) | async-done | bytes 4194320 | tf_op jit(solution)/shard_map/psum | solution.py:25
  550.2 11.7 %cholesky.222 = f32[128,128]{1,0:T(8,128)S(1)} custom-call(f32[128,128]{1,0:T(8,128)S(1)} %cholesky.577), custom_call_target="Cholesky" | custom-call | tf_op jit(solution)/shard_map/jit(cholesky)/cholesky | solution.py:27
  562.0 9.8 %custom-call.64 = f32[1,128,128]{1,2,0:T(8,128)S(1)} custom-call(f32[1,128,128]{2,1,0:T(8,128)S(1)} %get-tuple-element.56), custom_call_target="InvertDiagBlocksLowerTriangular" | custom-call | tf_op jit(solution)/shard_map/jit(cholesky)/cholesky | solution.py:27
  574.9 11.7 %cholesky.243 = f32[128,128]{1,0:T(8,128)S(1)} custom-call(f32[128,128]{1,0:T(8,128)S(1)} %cholesky.581), custom_call_target="Cholesky" | custom-call | tf_op jit(solution)/shard_map/jit(cholesky)/cholesky | solution.py:27
  589.7 9.8 %custom-call.65 = f32[1,128,128]{1,2,0:T(8,128)S(1)} custom-call(f32[1,128,128]{2,1,0:T(8,128)S(1)} %get-tuple-element.54), custom_call_target="InvertDiagBlocksLowerTriangular" | custom-call | tf_op jit(solution)/shard_map/jit(cholesky)/cholesky | solution.py:27
  605.1 11.7 %cholesky.466 = f32[128,128]{1,0:T(8,128)S(1)} custom-call(f32[128,128]{1,0:T(8,128)S(1)} %cholesky.586), custom_call_target="Cholesky" | custom-call | tf_op jit(solution)/shard_map/jit(cholesky)/cholesky | solution.py:27
  617.6 9.8 %custom-call.66 = f32[1,128,128]{1,2,0:T(8,128)S(1)} custom-call(f32[1,128,128]{2,1,0:T(8,128)S(1)} %get-tuple-element.52), custom_call_target="InvertDiagBlocksLowerTriangular" | custom-call | tf_op jit(solution)/shard_map/jit(cholesky)/cholesky | solution.py:27
  632.0 11.7 %cholesky.485 = f32[128,128]{1,0:T(8,128)S(1)} custom-call(f32[128,128]{1,0:T(8,128)S(1)} %cholesky.591), custom_call_target="Cholesky" | custom-call | tf_op jit(solution)/shard_map/jit(cholesky)/cholesky | solution.py:27
  658.6 12.1 %cholesky.504 = f32[128,128]{1,0:T(8,128)S(1)} custom-call(f32[128,128]{1,0:T(8,128)S(1)} %cholesky.596), custom_call_target="Cholesky" | custom-call | tf_op jit(solution)/shard_map/jit(cholesky)/cholesky | solution.py:27
  671.4 9.8 %custom-call.68 = f32[1,128,128]{1,2,0:T(8,128)S(1)} custom-call(f32[1,128,128]{2,1,0:T(8,128)S(1)} %get-tuple-element.48), custom_call_target="InvertDiagBlocksLowerTriangular" | custom-call | tf_op jit(solution)/shard_map/jit(cholesky)/cholesky | solution.py:27
  685.5 11.7 %cholesky.524 = f32[128,128]{1,0:T(8,128)S(1)} custom-call(f32[128,128]{1,0:T(8,128)S(1)} %cholesky.601), custom_call_target="Cholesky" | custom-call | tf_op jit(solution)/shard_map/jit(cholesky)/cholesky | solution.py:27
  698.0 9.8 %custom-call.69 = f32[1,128,128]{1,2,0:T(8,128)S(1)} custom-call(f32[1,128,128]{2,1,0:T(8,128)S(1)} %get-tuple-element.46), custom_call_target="InvertDiagBlocksLowerTriangular" | custom-call | tf_op jit(solution)/shard_map/jit(cholesky)/cholesky | solution.py:27
  711.6 11.7 %cholesky.544 = f32[128,128]{1,0:T(8,128)S(1)} custom-call(f32[128,128]{1,0:T(8,128)S(1)} %cholesky.606), custom_call_target="Cholesky" | custom-call | tf_op jit(solution)/shard_map/jit(cholesky)/cholesky | solution.py:27
  736.9 11.7 %cholesky.562 = f32[128,128]{1,0:T(8,128)S(1)} custom-call(f32[128,128]{1,0:T(8,128)S(1)} %convolution_subtract_fusion.6), custom_call_target="Cholesky" | custom-call | tf_op jit(solution)/shard_map/jit(cholesky)/cholesky | solution.py:27
  763.7 24.5 %while.1 = (s32[]{:T(128)}, f32[1024,1024]{0,1:T(8,128)}, s32[8,2]{0,1:T(2,128)S(1)}, f32[8,128,128]{2,1,0:T(8,128)S(1)}, s32[]{:T(128)}) while((s32[]{:T(128)}, f32[1024,1024]{0,1:T(8,128)}, s32[8,2]{0,1:T(2,128)S(1)}, f32[8,128,128]{2,1,0:T(8,128)S(1)}, s32[]{:T(128)}) %tuple.54), condition=%wide.while_cond, body=%wide.while_body.sunk | while | flops 2 | bytes 393321 | solution.py:29
  788.2 78.8 %custom-call.71 = f32[8,128,128]{1,2,0:T(8,128)S(1)} custom-call(f32[8,128,128]{2,1,0:T(8,128)S(1)} %get-tuple-element.16), custom_call_target="InvertDiagBlocksLowerTriangular" | custom-call | tf_op jit(solution)/shard_map/triangular_solve | solution.py:29
  (177 shorter events, 159.7 us)
Async XLA Ops:
  6.5 523.2 %all-reduce.4.cloned.1.call-start = ((), (), s32[]{:S(2)}) async-start(), calls=%async_computation.1 | async-start | bytes 8388608 | tf_op jit(solution)/shard_map/psum | solution.py:25
  340.6 3.2 copy-start.1
  548.3 2.0 copy-start.2
  867.0 21.1 %copy-start = (f32[1024,1024]{0,1:T(8,128)S(1)}, f32[1024,1024]{0,1:T(8,128)}, u32[]{:S(2)}) copy-start(f32[1024,1024]{0,1:T(8,128)} %all-reduce.4.cloned.1.call-done) | copy-start | bytes 12582916
Sparse Core Ops, SparseCore 0:
  360.8 168.8 all-reduce.3
where the time goes:
time: 912 us; the launch traced here: 905 us
  other arithmetic  279 us (31%)
  local copies, waits for them, and re-layouts  219 us (24%)
  blocking collectives  157 us (17%)
  waiting for transfers between devices  155 us (17%)
  matrix products  72.4 us (8%)
  between operations  21.5 us (2%)
    another operation x30, other arithmetic, shards(): jnp.linalg.cholesky(gram + shift * jnp.eye(samples, dtype=jnp.float32))  168 us
    psum x1, waiting for transfers between devices, shards(): gram = lax.psum(partial_gram, ('smp', 'col', 'slab'))  155 us
    unnamed x30, local copies, waits for them, and re-layouts  90.2 us
    all_to_all x1, blocking collectives, shards(): lax.all_to_all(jacobian, 'smp', split_axis=2, concat_axis=0, tiled=True)  86.4 us
    another operation x3, other arithmetic, shards(): lax.linalg.triangular_solve(factor, middle, left_side=True, lower=True, t...  83.7 us
    optimization_barrier x1, blocking collectives, shards(): jacobian, energies = lax.optimization_barrier((jacobian, energies))  70.8 us
    optimization_barrier x1, local copies, waits for them, and re-layouts, shards(): jacobian, energies = lax.optimization_barrier((jacobian, energies))  45.6 us
    convert_element_type x1, local copies, waits for them, and re-layouts, shards(): values = columns.astype(jnp.float32)  44 us
  transfers between devices with their start and end apart: 1, of which 1 were waited for; matrix products, arithmetic and copies ran while one was open for 1% of the time, Pallas kernels for 0%

commit v1 on v0

--- a/solution.py
+++ b/solution.py
@@ -22,7 +22,9 @@
         ((values - mean_row) / root_count).astype(jnp.bfloat16).reshape(samples, slab_count * width)
     )
     partial_gram = jnp.dot(centered, centered.T, preferred_element_type=jnp.float32)
-    gram = lax.psum(partial_gram, ("smp", "col", "slab"))
+    gram = partial_gram
+    for over in ("smp", ("col", "slab")):
+        gram = lax.psum(gram, over)
     shift = 0.01 * jnp.trace(gram) / samples
     factor = jnp.linalg.cholesky(gram + shift * jnp.eye(samples, dtype=jnp.float32))
     middle = lax.linalg.triangular_solve(factor, eps[:, None], left_side=True, lower=True)

time: 912 us -> 1240 us (1.36)
  waiting for transfers between devices: 155 us -> 487 us
    psum x1 -> x2, waiting for transfers between devices: 155 us -> 487 us  [shards(): gram = lax.psum(gram, over)]
  transfers between devices with their start and end apart: 1 -> 2, of which waited for: 1 -> 2; matrix products, arithmetic and copies ran while one was open for 1% -> 1% of each run, Pallas kernels for 0% -> 0%
where the time goes in v1:
time: 1240 us
  waiting for transfers between devices  487 us (39%)
  other arithmetic  279 us (22%)
  local copies, waits for them, and re-layouts  219 us (18%)
  blocking collectives  157 us (13%)
  matrix products  72.2 us (6%)
  between operations  21.6 us (2%)
    psum x2, waiting for transfers between devices, shards(): gram = lax.psum(gram, over)  487 us
    another operation x30, other arithmetic, shards(): jnp.linalg.cholesky(gram + shift * jnp.eye(samples, dtype=jnp.float32))  168 us
    unnamed x30, local copies, waits for them, and re-layouts  90.2 us
    all_to_all x1, blocking collectives, shards(): lax.all_to_all(jacobian, 'smp', split_axis=2, concat_axis=0, tiled=True)  86.4 us
    another operation x3, other arithmetic, shards(): lax.linalg.triangular_solve(factor, middle, left_side=True, lower=True, t...  83.7 us
    optimization_barrier x1, blocking collectives, shards(): jacobian, energies = lax.optimization_barrier((jacobian, energies))  70.8 us
    optimization_barrier x1, local copies, waits for them, and re-layouts, shards(): jacobian, energies = lax.optimization_barrier((jacobian, energies))  45.6 us
    convert_element_type x1, local copies, waits for them, and re-layouts, shards(): values = columns.astype(jnp.float32)  44 us
  transfers between devices with their start and end apart: 2, of which 2 were waited for; matrix products, arithmetic and copies ran while one was open for 1% of the time, Pallas kernels for 0%

profile of v1, /device:TPU:1, one launch (start us, length us, event | category | flops | bytes accessed | tf_op | source)
XLA Modules:
  0.0 1237.2 jit_solution(16327585318854223962)
XLA Ops:
  9.3 70.8 %all-reduce.1 = f32[1024]{0:T(1024)S(1)} all-reduce(f32[1024]{0:T(1024)S(1)} %dynamic-update-slice.47), channel_id=1, replica_groups=mesh['smp'=32,'col'=2,'slab'=2] {'smp'}, use_global_device_ids=true, to_apply=%add.1 | all-reduce | flops 1024 | bytes 8192 | tf_op jit(solution)/shard_map/optimization_barrier | solution.py:12
  80.1 45.6 %copy.65 = bf16[32,16,8192]{0,1,2:T(8,128)(2,1)} copy(bf16[32,16,8192]{2,1,0:T(8,128)(2,1)} %param.2) | data formatting | bytes 16777216 | tf_op jit(solution)/shard_map/optimization_barrier | solution.py:12
  125.7 39.8 %reshape.346 = bf16[32,2,65536]{2,1,0:T(2,128)(2,1)} reshape(bf16[8192,16,32]{2,1,0:T(8,128)(2,1)} %bitcast.343) | data formatting | bytes 16777216
  165.5 86.4 %all_to_all.4 = bf16[32,2,65536]{2,1,0:T(2,128)(2,1)} all-to-all(bf16[32,2,65536]{2,1,0:T(2,128)(2,1)} %reshape.346), channel_id=1, replica_groups=mesh['smp'=32,'col'=2,'slab'=2] {'smp'}, dimensions={0} | all-to-all | bytes 16777216 | tf_op jit(solution)/shard_map/all_to_all | solution.py:16
  251.9 30.6 %reshape.347 = bf16[8192,16,32]{2,1,0:T(8,128)(2,1)} reshape(bf16[32,2,65536]{2,1,0:T(2,128)(2,1)} %all_to_all.4) | data formatting | bytes 16777216
  282.5 44.0 %copy.66 = f32[32,16,32,256]{3,1,0,2:T(8,128)} copy(bf16[32,16,32,256]{0,1,3,2:T(8,128)(2,1)} %bitcast.342) | data formatting | bytes 25165824 | tf_op jit(solution)/shard_map/convert_element_type | solution.py:19
  343.8 16.6 %fusion.5 = f32[1024,1024]{0,1:T(8,128)} fusion(bf16[1024,16,256]{2,1,0:T(8,128)(2,1)S(1)} %bitcast.345), kind=kOutput, calls=%fused_computation.15 | convolution fusion | flops 8589934592 | bytes 12582912 | tf_op jit(solution)/shard_map/dot_general | solution.py:24
  360.7 318.0 %all-reduce.5.cloned.1.call-done = f32[1024,1024]{0,1:T(8,128)} async-done(((f32[1024,1024]{0,1:T(8,128)}), f32[1024,1024]{0,1:T(8,128)}) %all-reduce.5.cloned.1.call-update) | async-done | bytes 4194320 | tf_op jit(solution)/shard_map/psum | solution.py:27
  680.1 12.2 copy.98
  692.4 169.4 %all-reduce.7.cloned.1.call-done = f32[1024,1024]{0,1:T(8,128)} async-done(((f32[1024,1024]{0,1:T(8,128)}), f32[1024,1024]{0,1:T(8,128)}) %all-reduce.7.cloned.1.call-update) | async-done | bytes 4194320 | tf_op jit(solution)/shard_map/psum | solution.py:27
  882.3 11.7 cholesky.222
  894.1 9.8 custom-call.64
  907.0 11.7 cholesky.243
  921.8 9.8 custom-call.65
  937.1 11.7 cholesky.466
  949.6 9.8 custom-call.66
  964.0 11.7 cholesky.485
  976.5 9.8 custom-call.67
  990.6 12.1 cholesky.504
  1017.5 11.7 cholesky.524
  1043.7 11.7 cholesky.544
  1069.0 11.7 cholesky.562
  1095.8 24.5 %while.1 = (s32[]{:T(128)}, f32[1024,1024]{0,1:T(8,128)}, s32[8,2]{0,1:T(2,128)S(1)}, f32[8,128,128]{2,1,0:T(8,128)S(1)}, s32[]{:T(128)}) while((s32[]{:T(128)}, f32[1024,1024]{0,1:T(8,128)}, s32[8,2]{0,1:T(2,128)S(1)}, f32[8,128,128]{2,1,0:T(8,128)S(1)}, s32[]{:T(128)}) %tuple.54), condition=%wide.while_cond, body=%wide.while_body.sunk | while | flops 2 | bytes 393321 | solution.py:31
  1120.2 78.8 %custom-call.71 = f32[8,128,128]{1,2,0:T(8,128)S(1)} custom-call(f32[8,128,128]{2,1,0:T(8,128)S(1)} %get-tuple-element.16), custom_call_target="InvertDiagBlocksLowerTriangular" | custom-call | tf_op jit(solution)/shard_map/triangular_solve | solution.py:31
  (180 shorter events, 169.8 us)
Async XLA Ops:
  6.5 672.1 %all-reduce.5.cloned.1.call-start = ((), (), s32[]{:S(2)}) async-start(), calls=%async_computation.1 | async-start | bytes 8388608 | tf_op jit(solution)/shard_map/psum | solution.py:27
  340.6 3.2 copy-start.1
  360.4 501.4 %all-reduce.7.cloned.1.call-start = ((), (), s32[]{:S(2)}) async-start(), calls=%async_computation.2 | async-start | bytes 8388608 | tf_op jit(solution)/shard_map/psum | solution.py:27
  880.3 2.0 copy-start.2
  1199.1 21.1 %copy-start = (f32[1024,1024]{0,1:T(8,128)S(1)}, f32[1024,1024]{0,1:T(8,128)}, u32[]{:S(2)}) copy-start(f32[1024,1024]{0,1:T(8,128)} %all-reduce.7.cloned.1.call-done) | copy-start | bytes 12582916
Sparse Core Ops, SparseCore 0:
  360.6 318.0 all-reduce.4
  681.2 180.5 all-reduce.6
